TPU v7x, 32 devices: a whole 2x2x4 slice. The times are simulated.
32 devices in a mesh: dp: 2 (over y), row: 4 (over x, core), col: 4 (over z).
Axes of the slice: x: 2, y: 2, z: 4, core: 2. Of those that a mesh axis runs over, the one named last changes fastest.
Arguments:
- out_grad: float32 [128, 8192], P(('dp', 'row'), 'col'), parts along dimension 0, may hold values from -6 to 6
- hidden: float32 [128, 14336], P(('dp', 'col'), 'row'), parts along dimension 0, may hold values from -0.75 to 0.75
- weight: float32 [14336, 8192], P('row', 'col'), may hold values from -0.046875 to 0.046875
Outputs:
- weight_grad: float32 [28672, 8192], P(('dp', 'row'), 'col'), parts along dimension 0
- hidden_grad: float32 [128, 14336], P(('dp', 'col'), 'row'), parts along dimension 0
There are 2 independent parts, one for each index of `dp`. A program takes and returns all parts, laid end to end along the dimension named above; an argument that names none is the same for every part. Nothing has to cross between parts.
All inputs are finite; a program needn't handle non-finite values.
Results may differ from a plain program's by a relative error of at most 0.000071.
Values sent between devices are 32-bit elements; how exact they have to be, the bound alone decides.
A program may use at most 128 MiB of HBM per device.

v0:
```python
import jax
import jax.numpy as jnp
from jax import lax
from jax.sharding import PartitionSpec as P


def on_device(out_grad, hidden, weight):
    grad_all = lax.all_gather(out_grad, "row", axis=0, tiled=True)
    hidden_grad = lax.psum_scatter(
        lax.dot_general(
            grad_all,
            weight,
            (((1,), (1,)), ((), ())),
            precision=lax.Precision.HIGHEST,
            preferred_element_type=jnp.float32,
        ),
        "col",
        scatter_dimension=0,
        tiled=True,
    )
    hidden_all = lax.all_gather(hidden, "col", axis=0, tiled=True)
    weight_grad = lax.dot_general(
        hidden_all,
        grad_all,
        (((0,), (0,)), ((), ())),
        precision=lax.Precision.HIGHEST,
        preferred_element_type=jnp.float32,
    )
    return (weight_grad, hidden_grad)


def solution(mesh):
    placed = (P(("dp", "row"), "col"), P(("dp", "col"), "row"), P("row", "col"))
    return jax.shard_map(
        on_device,
        mesh=mesh,
        in_specs=placed,
        out_specs=(P(("dp", "row"), "col"), P(("dp", "col"), "row")),
        check_vma=False,
    )
```

profile of v0, /device:TPU:0, one launch (start us, length us, event | category | flops | bytes accessed | tf_op | source)
XLA Modules:
  0.0 114.4 jit_solution(8204558000565454148)
XLA Ops:
  7.2 0.0 copy-start
  7.2 0.0 reduce-scatter.2.cloned.1.call-start
  7.2 9.0 %all_gather.7 = f32[64,2048]{1,0:T(8,128)S(1)} all-gather(f32[16,2048]{1,0:T(8,128)} %param.3), channel_id=1, replica_groups=mesh['dp'=2,'row'=4,'col'=4] {'row'}, dimensions={0}, use_global_device_ids=true | all-gather | bytes 655360 | tf_op jit(solution)/shard_map/all_gather | solution.py:8
  16.2 32.0 %fusion.1 = f32[64,3584]{1,0:T(8,128)} fusion(f32[64,2048]{1,0:T(8,128)S(1)} %all_gather.7, f32[3584,2048]{1,0:T(8,128)} %param.5), kind=kOutput, calls=%fused_computation.1 | convolution fusion | flops 5637144576 | bytes 30801920 | tf_op jit(solution)/shard_map/dot_general | solution.py:10
  48.2 0.0 reduce-scatter.2.cloned.1.call-update
  48.2 0.0 copy-done
  48.2 32.5 %all_gather.6 = f32[64,3584]{1,0:T(8,128)S(1)} all-gather(f32[16,3584]{1,0:T(8,128)S(1)} %copy-done), channel_id=1, replica_groups=mesh['dp'=2,'row'=4,'col'=4] {'col'}, dimensions={0}, use_global_device_ids=true | all-gather | bytes 1146880 | tf_op jit(solution)/shard_map/all_gather | solution.py:21
  80.7 26.8 %fusion = f32[3584,2048]{1,0:T(8,128)} fusion(f32[64,3584]{1,0:T(8,128)S(1)} %all_gather.6, f32[64,2048]{1,0:T(8,128)S(1)} %all_gather.7), kind=kOutput, calls=%fused_computation | convolution fusion | flops 5637144576 | bytes 30801920 | tf_op jit(solution)/shard_map/dot_general | solution.py:22
  107.5 0.0 reduce-scatter.2.cloned.1.call-done
Async XLA Ops:
  7.2 41.0 %copy-start = (f32[16,3584]{1,0:T(8,128)S(1)}, f32[16,3584]{1,0:T(8,128)}, u32[]{:S(2)}) copy-start(f32[16,3584]{1,0:T(8,128)} %param.4) | copy-start | bytes 688132
  7.2 100.4 %reduce-scatter.2.cloned.1.call-start = ((), (), s32[]{:S(2)}) async-start(), calls=%async_computation.1 | async-start | bytes 1146880 | tf_op jit(solution)/shard_map/reduce_scatter | solution.py:9
Sparse Core Ops, SparseCore 0:
  48.3 35.3 reduce-scatter.1
where the time goes:
time: 115 us; the launch traced here: 114 us
  matrix products  58.8 us (51%)
  blocking collectives  41.5 us (36%)
  between operations  14 us (12%)
    all_gather x1, blocking collectives, on_device(): hidden_all = lax.all_gather(hidden, 'col', axis=0, tiled=True)  32.5 us
    dot_general x1, matrix products, on_device(): lax.dot_general(grad_all, weight, (((1,), (1,)), ((), ())), precision=lax...  32 us
    dot_general x1, matrix products, on_device(): lax.dot_general(hidden_all, grad_all, (((0,), (0,)), ((), ())), precision...  26.8 us
    all_gather x1, blocking collectives, on_device(): grad_all = lax.all_gather(out_grad, 'row', axis=0, tiled=True)  8.96 us
  transfers between devices with their start and end apart: 1, of which 0 were waited for; matrix products, arithmetic and copies ran while one was open for 23% of the time, Pallas kernels for 0%

commit v1 on v0

v1 whole, which is shorter than its diff:
```python
import functools

import jax
import jax.numpy as jnp
from jax import lax
from jax.experimental import pallas as pl
from jax.experimental.pallas import tpu as pltpu
from jax.sharding import PartitionSpec as P

MESH = pl.DeviceIdType.MESH
CHUNKS = 7


def split(x):
    high = x.astype(jnp.bfloat16)
    return high, (x - high.astype(jnp.float32)).astype(jnp.bfloat16)


def exchange(
    n_row, n_col, g_ref, h_ref, w_ref, g_all, h_all, out_ref,
    w_buf, g_parts, part, from_left, from_right,
    w_sem, own_sem, gx_send, gx_recv, gs_send, gs_recv,
    ag_send, ag_recv, rs_send, rs_recv,
):
    t, ff = h_ref.shape
    tg = g_ref.shape[0]
    width = ff // CHUNKS
    tokens = n_row * tg
    chips = n_row // 2
    row, z = lax.axis_index("row"), lax.axis_index("col")
    core = lax.rem(row, 2)
    chip = row // 2
    sibling = row + 1 - 2 * core
    not_first, not_last = z > 0, z < n_col - 1

    def w_copy(c):
        rows = pl.ds(c * width, width)
        return pltpu.make_async_copy(w_ref.at[rows], w_buf.at[rows], w_sem.at[c])

    for c in range(CHUNKS):
        w_copy(c).start()
    own_h = pltpu.make_async_copy(
        h_ref, h_all.at[pl.ds(pl.multiple_of(z * t, t), t)], own_sem.at[0]
    )
    own_g = pltpu.make_async_copy(
        g_ref, g_all.at[pl.ds(pl.multiple_of(row * tg, tg), tg)], own_sem.at[1]
    )
    own_h.start()
    own_g.start()

    barrier = pltpu.get_barrier_semaphore()

    def greet(where):
        pl.semaphore_signal(barrier, inc=1, device_id=where, device_id_type=MESH)

    def peer(k):
        return lax.rem(chip + k, chips) * 2 + core

    for k in range(1, chips):
        greet({"row": peer(k)})
    greet({"row": sibling})

    @pl.when(not_first)
    def _():
        greet({"col": z - 1})

    @pl.when(not_last)
    def _():
        greet({"col": z + 1})

    pl.semaphore_wait(
        barrier, chips + not_first.astype(jnp.int32) + not_last.astype(jnp.int32)
    )

    def g_rows(r):
        return g_all.at[pl.ds(pl.multiple_of(r * tg, tg), tg)]

    def across(k):
        return pltpu.make_async_remote_copy(
            g_ref, g_rows(row), gx_send.at[k - 1], gx_recv.at[k - 1],
            device_id={"row": peer(k)}, device_id_type=MESH,
        )

    def arrived(k):
        source = lax.rem(chip + chips - k, chips) * 2 + core
        return pltpu.make_async_remote_copy(
            g_ref, g_rows(source), gx_send.at[k - 1], gx_recv.at[k - 1],
            device_id={"row": source}, device_id_type=MESH,
        )

    def aside(k, mine):
        owner = lax.rem(chip + chips - k, chips) * 2 + (core if mine else 1 - core)
        return pltpu.make_async_remote_copy(
            g_ref if k == 0 and mine else g_rows(owner), g_rows(owner),
            gs_send.at[k], gs_recv.at[k],
            device_id={"row": sibling}, device_id_type=MESH,
        )

    for k in range(1, chips):
        across(k).start()
    aside(0, True).start()

    def ag(flow, hop, c, shard):
        cols = pl.ds(pl.multiple_of(c * width, width), width)
        rows = pl.ds(pl.multiple_of(shard * t, t), t)
        source = h_ref.at[:, cols] if hop is None else h_all.at[rows, cols]
        index = c if hop is None else hop * CHUNKS + c
        return pltpu.make_async_remote_copy(
            source, h_all.at[rows, cols],
            ag_send.at[flow, index], ag_recv.at[flow, index],
            device_id={"col": z + 1 - 2 * flow}, device_id_type=MESH,
        )

    def going(flow):
        return not_first if flow else not_last

    for c in range(CHUNKS):
        for flow in range(2):

            @pl.when(going(flow))
            def _():
                ag(flow, None, c, z).start()

    def pass_on(hop, c):
        for flow in range(2):
            shard = z + hop if flow else z - hop
            there = (shard < n_col) if flow else (shard >= 0)

            @pl.when(there)
            def _():
                ag(flow, hop - 1, c, shard).wait_recv()

            @pl.when(there & going(flow))
            def _():
                ag(flow, hop, c, shard).start()

    half = CHUNKS // 2
    for c in range(half):
        pass_on(1, c)
    for k in range(1, chips):
        arrived(k).wait_recv()
        aside(k, True).start()
    for c in range(half, CHUNKS):
        pass_on(1, c)
    for k in range(chips):
        aside(k, False).wait_recv()
    own_g.wait()
    own_h.wait()
    high, low = split(g_all[...])
    g_parts[pl.ds(0, tokens)] = high
    g_parts[pl.ds(tokens, tokens)] = low

    def rs(flow, d, c):
        held = from_right if flow else from_left
        view = held.at[pl.ds(d * t, t), pl.ds(pl.multiple_of(c * width, width), width)]
        index = d * CHUNKS + c
        return pltpu.make_async_remote_copy(
            view, view, rs_send.at[flow, index], rs_recv.at[flow, index],
            device_id={"col": z + 1 - 2 * flow}, device_id_type=MESH,
        )

    def sums(flow, c):
        held = from_right if flow else from_left
        cols = pl.ds(pl.multiple_of(c * width, width), width)
        first = (z == n_col - 1) if flow else (z == 0)
        for d in range(n_col) if flow else range(n_col - 1, -1, -1):
            rows = pl.ds(d * t, t)
            on = (d < z) if flow else (d > z)

            @pl.when(jnp.logical_not(first) & (on | (z == d)))
            def _():
                rs(flow, d, c).wait_recv()

            @pl.when(on & first)
            def _():
                held[rows, cols] = part[rows, cols]

            @pl.when(on & jnp.logical_not(first))
            def _():
                held[rows, cols] += part[rows, cols]

            @pl.when(on)
            def _():
                rs(flow, d, c).start()

    contract = (((1,), (1,)), ((), ()))

    def step(i, carry):
        @pl.when(i < CHUNKS)
        def _():
            c = i
            w_copy(c).wait()
            at = pl.ds(pl.multiple_of(c * width, width), width)
            w_high, w_low = split(w_buf[at, :])
            both = lax.dot_general(
                g_parts[...], w_high, contract, preferred_element_type=jnp.float32
            )
            rest = lax.dot_general(
                g_parts[pl.ds(0, tokens)], w_low, contract,
                preferred_element_type=jnp.float32,
            )
            part[:, at] = both[:tokens] + (both[tokens:] + rest)

        for flow in range(2):
            c = i - (n_col - 1 - z if flow else z)

            @pl.when((c >= 0) & (c < CHUNKS))
            def _():
                sums(flow, c)

        @pl.when(i < (n_col - 2) * CHUNKS)
        def _():
            pass_on(i // CHUNKS + 2, lax.rem(i, CHUNKS))

        return carry

    lax.fori_loop(0, max(CHUNKS + n_col - 1, (n_col - 2) * CHUNKS), step, 0)

    mine = pl.ds(pl.multiple_of(z * t, t), t)
    out_ref[...] = part[mine]

    @pl.when(not_first)
    def _():
        out_ref[...] += from_left[mine]

    @pl.when(not_last)
    def _():
        out_ref[...] += from_right[mine]

    for k in range(1, chips):
        across(k).wait_send()
    for k in range(chips):
        aside(k, True).wait_send()

    def drain(c, carry):
        for flow in range(2):

            @pl.when(going(flow))
            def _():
                ag(flow, None, c, z).wait_send()

            for hop in range(1, n_col - 1):
                shard = z + hop if flow else z - hop
                there = (shard < n_col) if flow else (shard >= 0)

                @pl.when(there & going(flow))
                def _():
                    ag(flow, hop, c, shard).wait_send()

            for d in range(n_col):

                @pl.when((d < z) if flow else (d > z))
                def _():
                    rs(flow, d, c).wait_send()

        return carry

    lax.fori_loop(0, CHUNKS, drain, 0)


def outer(tile, h_ref, g_ref, out_ref, g_parts):
    tokens = g_ref.shape[0]

    @pl.when(pl.program_id(0) == 0)
    def _():
        high, low = split(g_ref[...])
        g_parts[pl.ds(0, tokens)] = high
        g_parts[pl.ds(tokens, tokens)] = low
        g_parts[pl.ds(2 * tokens, tokens)] = high

    at = pl.ds(pl.multiple_of(pl.program_id(0) * tile, tile), tile)
    high, low = split(h_ref[:, at])
    out_ref[...] = lax.dot_general(
        jnp.concatenate([high, high, low], axis=0), g_parts[...],
        (((0,), (0,)), ((), ())), preferred_element_type=jnp.float32,
    )


def on_device(n_row, n_col, out_grad, hidden, weight):
    f32 = jnp.float32
    (tg, d), (t, ff) = out_grad.shape, hidden.shape
    tokens = n_row * tg
    dma = pltpu.SemaphoreType.DMA
    whole = pl.BlockSpec(memory_space=pltpu.VMEM)
    chips = n_row // 2
    g_all, h_all, hidden_grad = pl.pallas_call(
        functools.partial(exchange, n_row, n_col),
        out_shape=(
            jax.ShapeDtypeStruct((tokens, d), f32),
            jax.ShapeDtypeStruct((tokens, ff), f32),
            jax.ShapeDtypeStruct((t, ff), f32),
        ),
        in_specs=[pl.BlockSpec(memory_space=pl.ANY)] * 3,
        out_specs=(whole,) * 3,
        scratch_shapes=[
            pltpu.VMEM((ff, d), f32),
            pltpu.VMEM((2 * tokens, d), jnp.bfloat16),
            pltpu.VMEM((tokens, ff), f32),
            pltpu.VMEM((tokens, ff), f32),
            pltpu.VMEM((tokens, ff), f32),
            dma((CHUNKS,)),
            dma((2,)),
            dma((max(chips - 1, 1),)),
            dma((max(chips - 1, 1),)),
            dma((chips,)),
            dma((chips,)),
            dma((2, (n_col - 1) * CHUNKS)),
            dma((2, (n_col - 1) * CHUNKS)),
            dma((2, n_col * CHUNKS)),
            dma((2, n_col * CHUNKS)),
        ],
        compiler_params=pltpu.CompilerParams(
            collective_id=0, has_side_effects=True, vmem_limit_bytes=56 << 20
        ),
        name="exchange",
    )(out_grad, hidden, weight)
    tile = 256 if ff % 256 == 0 and ff > 1024 else 128
    weight_grad = pl.pallas_call(
        functools.partial(outer, tile),
        grid=(ff // tile,),
        out_shape=jax.ShapeDtypeStruct((ff, d), f32),
        in_specs=[whole, whole],
        out_specs=pl.BlockSpec((tile, d), lambda i: (i, 0)),
        scratch_shapes=[pltpu.VMEM((3 * tokens, d), jnp.bfloat16)],
        compiler_params=pltpu.CompilerParams(vmem_limit_bytes=40 << 20),
        name="outer",
    )(h_all, g_all)
    return (weight_grad, hidden_grad)


def solution(mesh):
    placed = (P(("dp", "row"), "col"), P(("dp", "col"), "row"), P("row", "col"))
    return jax.shard_map(
        functools.partial(on_device, mesh.shape["row"], mesh.shape["col"]),
        mesh=mesh,
        in_specs=placed,
        out_specs=(P(("dp", "row"), "col"), P(("dp", "col"), "row")),
        check_vma=False,
    )
```

time: 115 us -> 61.1 us (0.53)
  matrix products: 58.8 us -> 0 us
  Pallas kernels: 0 us -> 57.3 us
  blocking collectives: 41.5 us -> 0 us
  between operations: 14 us -> 0.65 us
  local copies, waits for them, and re-layouts: 0.01 us -> 2.9 us
    dot_general x2 -> x0, matrix products: 58.8 us -> none  [the longest x1 32 us: on_device(): lax.dot_general(grad_all, weight, (((1,), (1,)), ((), ())), precision=lax...]
    pallas_call x0 -> x2, Pallas kernels: none -> 57.3 us  [the longest x1 44.1 us: on_device(): pl.pallas_call(functools.partial(exchange, n_row, n_col), out_shape=(jax....]
    all_gather x2 -> x0, blocking collectives: 41.5 us -> none  [the longest x1 32.5 us: on_device(): hidden_all = lax.all_gather(hidden, 'col', axis=0, tiled=True)]
    unnamed x2 -> x7, local copies, waits for them, and re-layouts: 0.01 us -> 2.9 us
  transfers between devices with their start and end apart: 1 -> 0, of which waited for: 0 -> 0; matrix products, arithmetic and copies ran while one was open for 23% -> 0% of each run, Pallas kernels for 0% -> 0%
where the time goes in v1:
time: 61.1 us; the launch traced here: 60.9 us
  Pallas kernels  57.3 us (94%)
  local copies, waits for them, and re-layouts  2.9 us (5%)
  between operations  0.65 us (1%)
    pallas_call x1, Pallas kernels, on_device(): pl.pallas_call(functools.partial(exchange, n_row, n_col), out_shape=(jax....  44.1 us
    pallas_call x1, Pallas kernels, on_device(): pl.pallas_call(functools.partial(outer, tile), grid=(ff // tile,), out_sh...  13.3 us
    unnamed x7, local copies, waits for them, and re-layouts  2.9 us

profile of v1, /device:TPU:0, one launch (start us, length us, event | category | flops | bytes accessed | tf_op | source)
XLA Modules:
  0.0 60.9 jit_solution(6615178585875020801)
XLA Ops:
  0.6 44.1 %exchange.1 = (f32[64,2048]{1,0:T(8,128)}, f32[64,3584]{1,0:T(8,128)}, f32[16,3584]{1,0:T(8,128)}) custom-call(f32[16,2048]{1,0:T(8,128)} %g_ref.1, f32[16,3584]{1,0:T(8,128)} %h_ref.1, f32[3584,2048]{1,0:T(8,128)} %w_ref.1), custom_call_target="tpu_custom_call" | custom-call | tf_op jit(solution)/shard_map/exchange/pallas_call | solution.py:286
  44.7 0.0 copy-start
  44.7 1.2 %copy-done = f32[64,3584]{1,0:T(8,128)S(1)} copy-done((f32[64,3584]{1,0:T(8,128)S(1)}, f32[64,3584]{1,0:T(8,128)}, u32[]{:S(2)}) %copy-start) | copy-done | bytes 917528
  45.9 0.0 copy-start.1
  45.9 1.0 %copy-done.1 = f32[64,2048]{1,0:T(8,128)S(1)} copy-done((f32[64,2048]{1,0:T(8,128)S(1)}, f32[64,2048]{1,0:T(8,128)}, u32[]{:S(2)}) %copy-start.1) | copy-done | bytes 524312
  46.9 0.0 copy-start.2
  46.9 13.3 %outer.1 = f32[3584,2048]{1,0:T(8,128)} custom-call(f32[64,3584]{1,0:T(8,128)S(1)} %copy-done, f32[64,2048]{1,0:T(8,128)S(1)} %copy-done.1), custom_call_target="tpu_custom_call" | custom-call | tf_op jit(solution)/shard_map/outer/pallas_call | solution.py:318
  60.2 0.0 copy-done.2
  60.2 0.7 %copy.6 = f32[16,3584]{1,0:T(8,128)} copy(f32[16,3584]{1,0:T(8,128)S(1)} %copy-done.2) | data formatting | bytes 458752
Async XLA Ops:
  44.7 1.2 %copy-start = (f32[64,3584]{1,0:T(8,128)S(1)}, f32[64,3584]{1,0:T(8,128)}, u32[]{:S(2)}) copy-start(f32[64,3584]{1,0:T(8,128)} %get-tuple-element.5.h_ref) | copy-start | bytes 2752516
  45.9 1.0 %copy-start.1 = (f32[64,2048]{1,0:T(8,128)S(1)}, f32[64,2048]{1,0:T(8,128)}, u32[]{:S(2)}) copy-start(f32[64,2048]{1,0:T(8,128)} %get-tuple-element.6.g_ref) | copy-start | bytes 1572868
  46.9 13.3 %copy-start.2 = (f32[16,3584]{1,0:T(8,128)S(1)}, f32[16,3584]{1,0:T(8,128)}, u32[]{:S(2)}) copy-start(f32[16,3584]{1,0:T(8,128)} %get-tuple-element.11) | copy-start | bytes 688132

commit v2 on v1

--- a/solution.py
+++ b/solution.py
@@ -9,6 +9,8 @@
 
 MESH = pl.DeviceIdType.MESH
 CHUNKS = 7
+LAG = 2
+PASSES = 2
 
 
 def split(x):
@@ -17,8 +19,8 @@
 
 
 def exchange(
-    n_row, n_col, g_ref, h_ref, w_ref, g_all, h_all, out_ref,
-    w_buf, g_parts, part, from_left, from_right,
+    n_row, n_col, g_ref, h_ref, w_ref, g_out, h_out, out_ref,
+    g_all, h_all, w_buf, g_parts, part, from_left, from_right,
     w_sem, own_sem, gx_send, gx_recv, gs_send, gs_recv,
     ag_send, ag_recv, rs_send, rs_recv,
 ):
@@ -149,6 +151,9 @@
     high, low = split(g_all[...])
     g_parts[pl.ds(0, tokens)] = high
     g_parts[pl.ds(tokens, tokens)] = low
+    give_g = pltpu.make_async_copy(g_all, g_out, own_sem.at[0])
+    give_h = pltpu.make_async_copy(h_all, h_out, own_sem.at[1])
+    give_g.start()
 
     def rs(flow, d, c):
         held = from_right if flow else from_left
@@ -184,6 +189,9 @@
                 rs(flow, d, c).start()
 
     contract = (((1,), (1,)), ((), ()))
+
+    items = (n_col - 2) * CHUNKS
+    passes = -(-items // PASSES)
 
     def step(i, carry):
         @pl.when(i < CHUNKS)
@@ -201,20 +209,27 @@
             )
             part[:, at] = both[:tokens] + (both[tokens:] + rest)
 
+        for k in range(PASSES):
+            item = PASSES * i + k
+
+            @pl.when(item < items)
+            def _():
+                pass_on(item // CHUNKS + 2, lax.rem(item, CHUNKS))
+
+        @pl.when(i == passes - 1)
+        def _():
+            give_h.start()
+
         for flow in range(2):
-            c = i - (n_col - 1 - z if flow else z)
+            c = i - LAG * (n_col - 1 - z if flow else z)
 
             @pl.when((c >= 0) & (c < CHUNKS))
             def _():
                 sums(flow, c)
 
-        @pl.when(i < (n_col - 2) * CHUNKS)
-        def _():
-            pass_on(i // CHUNKS + 2, lax.rem(i, CHUNKS))
-
         return carry
 
-    lax.fori_loop(0, max(CHUNKS + n_col - 1, (n_col - 2) * CHUNKS), step, 0)
+    lax.fori_loop(0, max(CHUNKS + LAG * (n_col - 1), passes), step, 0)
 
     mine = pl.ds(pl.multiple_of(z * t, t), t)
     out_ref[...] = part[mine]
@@ -256,24 +271,50 @@
         return carry
 
     lax.fori_loop(0, CHUNKS, drain, 0)
-
-
-def outer(tile, h_ref, g_ref, out_ref, g_parts):
-    tokens = g_ref.shape[0]
-
-    @pl.when(pl.program_id(0) == 0)
-    def _():
-        high, low = split(g_ref[...])
-        g_parts[pl.ds(0, tokens)] = high
-        g_parts[pl.ds(tokens, tokens)] = low
-        g_parts[pl.ds(2 * tokens, tokens)] = high
-
-    at = pl.ds(pl.multiple_of(pl.program_id(0) * tile, tile), tile)
-    high, low = split(h_ref[:, at])
-    out_ref[...] = lax.dot_general(
-        jnp.concatenate([high, high, low], axis=0), g_parts[...],
-        (((0,), (0,)), ((), ())), preferred_element_type=jnp.float32,
-    )
+    give_g.wait()
+    give_h.wait()
+
+
+def outer(
+    tile, h_ref, g_ref, hg_ref, out_ref, hg_out,
+    h_buf, g_buf, g_parts, buf, in_sem, out_sem,
+):
+    tokens, ff = h_ref.shape
+    width = ff // CHUNKS
+    moved = pltpu.make_async_copy(hg_ref, hg_out, in_sem.at[CHUNKS + 1])
+    g_in = pltpu.make_async_copy(g_ref, g_buf, in_sem.at[CHUNKS])
+    g_in.start()
+
+    def h_in(c):
+        at = pl.ds(c * width, width)
+        return pltpu.make_async_copy(h_ref.at[:, at], h_buf.at[:, at], in_sem.at[c])
+
+    for c in range(CHUNKS):
+        h_in(c).start()
+    moved.start()
+    g_in.wait()
+    high, low = split(g_buf[...])
+    g_parts[pl.ds(0, tokens)] = high
+    g_parts[pl.ds(tokens, tokens)] = low
+    g_parts[pl.ds(2 * tokens, tokens)] = high
+
+    def give(i):
+        at = pl.ds(i * tile, tile)
+        return pltpu.make_async_copy(buf.at[at], out_ref.at[at], out_sem.at[i])
+
+    for i in range(ff // tile):
+        if i * tile % width == 0:
+            h_in(i * tile // width).wait()
+        at = pl.ds(i * tile, tile)
+        high, low = split(h_buf[:, at])
+        buf[at] = lax.dot_general(
+            jnp.concatenate([high, high, low], axis=0), g_parts[...],
+            (((0,), (0,)), ((), ())), preferred_element_type=jnp.float32,
+        )
+        give(i).start()
+    for i in range(ff // tile):
+        give(i).wait()
+    moved.wait()
 
 
 def on_device(n_row, n_col, out_grad, hidden, weight):
@@ -282,6 +323,7 @@
     tokens = n_row * tg
     dma = pltpu.SemaphoreType.DMA
     whole = pl.BlockSpec(memory_space=pltpu.VMEM)
+    anywhere = pl.BlockSpec(memory_space=pltpu.HBM)
     chips = n_row // 2
     g_all, h_all, hidden_grad = pl.pallas_call(
         functools.partial(exchange, n_row, n_col),
@@ -290,9 +332,11 @@
             jax.ShapeDtypeStruct((tokens, ff), f32),
             jax.ShapeDtypeStruct((t, ff), f32),
         ),
-        in_specs=[pl.BlockSpec(memory_space=pl.ANY)] * 3,
-        out_specs=(whole,) * 3,
+        in_specs=[anywhere] * 3,
+        out_specs=(anywhere, anywhere, whole),
         scratch_shapes=[
+            pltpu.VMEM((tokens, d), f32),
+            pltpu.VMEM((tokens, ff), f32),
             pltpu.VMEM((ff, d), f32),
             pltpu.VMEM((2 * tokens, d), jnp.bfloat16),
             pltpu.VMEM((tokens, ff), f32),
@@ -315,16 +359,25 @@
         name="exchange",
     )(out_grad, hidden, weight)
     tile = 256 if ff % 256 == 0 and ff > 1024 else 128
-    weight_grad = pl.pallas_call(
+    weight_grad, hidden_grad = pl.pallas_call(
         functools.partial(outer, tile),
-        grid=(ff // tile,),
-        out_shape=jax.ShapeDtypeStruct((ff, d), f32),
-        in_specs=[whole, whole],
-        out_specs=pl.BlockSpec((tile, d), lambda i: (i, 0)),
-        scratch_shapes=[pltpu.VMEM((3 * tokens, d), jnp.bfloat16)],
-        compiler_params=pltpu.CompilerParams(vmem_limit_bytes=40 << 20),
+        out_shape=(
+            jax.ShapeDtypeStruct((ff, d), f32),
+            jax.ShapeDtypeStruct((t, ff), f32),
+        ),
+        in_specs=[anywhere] * 3,
+        out_specs=(anywhere,) * 2,
+        scratch_shapes=[
+            pltpu.VMEM((tokens, ff), f32),
+            pltpu.VMEM((tokens, d), f32),
+            pltpu.VMEM((3 * tokens, d), jnp.bfloat16),
+            pltpu.VMEM((ff, d), f32),
+            dma((CHUNKS + 2,)),
+            dma((ff // tile,)),
+        ],
+        compiler_params=pltpu.CompilerParams(vmem_limit_bytes=56 << 20),
         name="outer",
-    )(h_all, g_all)
+    )(h_all, g_all, hidden_grad)
     return (weight_grad, hidden_grad)
 
 

time: 61.1 us -> 50.5 us (0.83)
  Pallas kernels: 57.3 us -> 49.7 us
  local copies, waits for them, and re-layouts: 2.9 us -> 0 us
    pallas_call x1, Pallas kernels: 44.1 us -> 38.3 us  [on_device(): pl.pallas_call(functools.partial(exchange, n_row, n_col), out_shape=(jax....]
    unnamed x7 -> x0, local copies, waits for them, and re-layouts: 2.9 us -> none
    pallas_call x1, Pallas kernels: 13.3 us -> 11.4 us  [on_device(): pl.pallas_call(functools.partial(outer, tile), out_shape=(jax.ShapeDtypeS...]
where the time goes in v2:
time: 50.5 us; the launch traced here: 50.4 us
  Pallas kernels  49.7 us (98%)
  between operations  0.64 us (1%)
    pallas_call x1, Pallas kernels, on_device(): pl.pallas_call(functools.partial(exchange, n_row, n_col), out_shape=(jax....  38.3 us
    pallas_call x1, Pallas kernels, on_device(): pl.pallas_call(functools.partial(outer, tile), out_shape=(jax.ShapeDtypeS...  11.4 us

profile of v2, /device:TPU:0, one launch (start us, length us, event | category | flops | bytes accessed | tf_op | source)
XLA Modules:
  0.0 50.4 jit_solution(1528097767659237131)
XLA Ops:
  0.6 38.3 %exchange.1 = (f32[64,2048]{1,0:T(8,128)}, f32[64,3584]{1,0:T(8,128)}, f32[16,3584]{1,0:T(8,128)}) custom-call(f32[16,2048]{1,0:T(8,128)} %g_ref.1, f32[16,3584]{1,0:T(8,128)} %h_ref.1, f32[3584,2048]{1,0:T(8,128)} %w_ref.1), custom_call_target="tpu_custom_call" | custom-call | tf_op jit(solution)/shard_map/exchange/pallas_call | solution.py:328
  39.0 11.4 %outer.1 = (f32[3584,2048]{1,0:T(8,128)}, f32[16,3584]{1,0:T(8,128)}) custom-call(f32[64,3584]{1,0:T(8,128)} %get-tuple-element.5.h_ref, f32[64,2048]{1,0:T(8,128)} %get-tuple-element.6.g_ref, f32[16,3584]{1,0:T(8,128)} %get-tuple-element.7.hg_ref), custom_call_target="tpu_custom_call" | custom-call | tf_op jit(solution)/shard_map/outer/pallas_call | solution.py:362

commit v3 on v2

--- a/solution.py
+++ b/solution.py
@@ -20,9 +20,9 @@
 
 def exchange(
     n_row, n_col, g_ref, h_ref, w_ref, g_out, h_out, out_ref,
-    g_all, h_all, w_buf, g_parts, part, from_left, from_right,
+    g_all, h_all, w_buf, g_parts, part, from_left, from_right, near,
     w_sem, own_sem, gx_send, gx_recv, gs_send, gs_recv,
-    ag_send, ag_recv, rs_send, rs_recv,
+    ag_send, ag_recv, rs_send, rs_recv, near_send, near_recv,
 ):
     t, ff = h_ref.shape
     tg = g_ref.shape[0]
@@ -62,17 +62,9 @@
         greet({"row": peer(k)})
     greet({"row": sibling})
 
-    @pl.when(not_first)
-    def _():
-        greet({"col": z - 1})
-
-    @pl.when(not_last)
-    def _():
-        greet({"col": z + 1})
-
-    pl.semaphore_wait(
-        barrier, chips + not_first.astype(jnp.int32) + not_last.astype(jnp.int32)
-    )
+    for k in range(1, n_col):
+        greet({"col": lax.rem(z + k, n_col)})
+    pl.semaphore_wait(barrier, chips + n_col - 1)
 
     def g_rows(r):
         return g_all.at[pl.ds(pl.multiple_of(r * tg, tg), tg)]
@@ -188,6 +180,17 @@
             def _():
                 rs(flow, d, c).start()
 
+    last = (CHUNKS - 1) * width
+
+    def straight(k):
+        owner = lax.rem(z + k, n_col)
+        rows = pl.ds(pl.multiple_of(owner * t, t), t)
+        return pltpu.make_async_remote_copy(
+            part.at[rows, pl.ds(last, width)], near.at[k - 1],
+            near_send.at[k - 1], near_recv.at[k - 1],
+            device_id={"col": owner}, device_id_type=MESH,
+        )
+
     contract = (((1,), (1,)), ((), ()))
 
     items = (n_col - 2) * CHUNKS
@@ -209,6 +212,11 @@
             )
             part[:, at] = both[:tokens] + (both[tokens:] + rest)
 
+        @pl.when(i == CHUNKS - 1)
+        def _():
+            for k in range(1, n_col):
+                straight(k).start()
+
         for k in range(PASSES):
             item = PASSES * i + k
 
@@ -223,7 +231,7 @@
         for flow in range(2):
             c = i - LAG * (n_col - 1 - z if flow else z)
 
-            @pl.when((c >= 0) & (c < CHUNKS))
+            @pl.when((c >= 0) & (c < CHUNKS - 1))
             def _():
                 sums(flow, c)
 
@@ -236,11 +244,17 @@
 
     @pl.when(not_first)
     def _():
-        out_ref[...] += from_left[mine]
+        out_ref[:, pl.ds(0, last)] += from_left[mine, pl.ds(0, last)]
 
     @pl.when(not_last)
     def _():
-        out_ref[...] += from_right[mine]
+        out_ref[:, pl.ds(0, last)] += from_right[mine, pl.ds(0, last)]
+
+    for k in range(1, n_col):
+        straight(k).wait_recv()
+        out_ref[:, pl.ds(last, width)] += near[k - 1]
+    for k in range(1, n_col):
+        straight(k).wait_send()
 
     for k in range(1, chips):
         across(k).wait_send()
@@ -264,7 +278,7 @@
 
             for d in range(n_col):
 
-                @pl.when((d < z) if flow else (d > z))
+                @pl.when((c < CHUNKS - 1) & ((d < z) if flow else (d > z)))
                 def _():
                     rs(flow, d, c).wait_send()
 
@@ -342,6 +356,7 @@
             pltpu.VMEM((tokens, ff), f32),
             pltpu.VMEM((tokens, ff), f32),
             pltpu.VMEM((tokens, ff), f32),
+            pltpu.VMEM((n_col - 1, t, ff // CHUNKS), f32),
             dma((CHUNKS,)),
             dma((2,)),
             dma((max(chips - 1, 1),)),
@@ -352,6 +367,8 @@
             dma((2, (n_col - 1) * CHUNKS)),
             dma((2, n_col * CHUNKS)),
             dma((2, n_col * CHUNKS)),
+            dma((n_col - 1,)),
+            dma((n_col - 1,)),
         ],
         compiler_params=pltpu.CompilerParams(
             collective_id=0, has_side_effects=True, vmem_limit_bytes=56 << 20

time: 50.5 us -> 50.9 us (level)
  no operation moved by 1% of the time
where the time goes in v3:
time: 50.9 us; the launch traced here: 50.7 us
  Pallas kernels  50.1 us (98%)
  between operations  0.64 us (1%)
    pallas_call x1, Pallas kernels, on_device(): pl.pallas_call(functools.partial(exchange, n_row, n_col), out_shape=(jax....  38.7 us
    pallas_call x1, Pallas kernels, on_device(): pl.pallas_call(functools.partial(outer, tile), out_shape=(jax.ShapeDtypeS...  11.4 us

profile of v3, /device:TPU:0, one launch (start us, length us, event | category | flops | bytes accessed | tf_op | source)
XLA Modules:
  0.0 50.7 jit_solution(15418357830698609893)
XLA Ops:
  0.6 38.7 %exchange.1 = (f32[64,2048]{1,0:T(8,128)}, f32[64,3584]{1,0:T(8,128)}, f32[16,3584]{1,0:T(8,128)}) custom-call(f32[16,2048]{1,0:T(8,128)} %g_ref.1, f32[16,3584]{1,0:T(8,128)} %h_ref.1, f32[3584,2048]{1,0:T(8,128)} %w_ref.1), custom_call_target="tpu_custom_call" | custom-call | tf_op jit(solution)/shard_map/exchange/pallas_call | solution.py:342
  39.3 11.4 %outer.1 = (f32[3584,2048]{1,0:T(8,128)}, f32[16,3584]{1,0:T(8,128)}) custom-call(f32[64,3584]{1,0:T(8,128)} %get-tuple-element.5.h_ref, f32[64,2048]{1,0:T(8,128)} %get-tuple-element.6.g_ref, f32[16,3584]{1,0:T(8,128)} %get-tuple-element.7.hg_ref), custom_call_target="tpu_custom_call" | custom-call | tf_op jit(solution)/shard_map/outer/pallas_call | solution.py:379
